TPU v7x, 32 devices: a whole 2x2x4 slice. The times are simulated.
32 devices in a mesh: range: 8 (over z, y), alt: 4 (over x, core), freq: 1.
Axes of the slice: x: 2, y: 2, z: 4, core: 2. Of those that a mesh axis runs over, the one named last changes fastest.
Arguments:
- freq_scale: float32 [2], P('freq'), may hold values from 1 to 2
- base_profile: float32 [1024], P('alt'), may hold values from 1.5 to 3
- perturb: float32 [32, 1024], P('range', 'alt'), may hold values from -1 to 1
- start_block: float32 [96, 1024], P(None, 'alt'), may hold values from -6 to 6
- source: float32 [2, 2, 96], P('freq'), may hold values from -6 to 6
Outputs:
- field: float32 [2, 32, 2, 1024], P('freq', 'range', None, 'alt')
All inputs are finite; a program needn't handle non-finite values.
Results may differ from a plain program's by a relative error of at most 0.0003.
Values sent between devices are 32-bit elements; how exact they have to be, the bound alone decides.
No kernel may reach another device: no remote copies, remote signals or barrier semaphores. Data moves between devices by JAX's collectives and lax.ppermute only.
A program may use at most 128 MiB of HBM per device.

v0:
```python
import jax
import jax.numpy as jnp
from jax import lax
from jax.sharding import PartitionSpec as P

ITERS = 8
phase_step = 0.15
relief = 0.1


def with_halo(block, sides, width):
    for axis, dim in sides:
        count = lax.axis_size(axis)
        forward = [(i, i + 1) for i in range(count - 1)]
        backward = [(target, source) for source, target in forward]
        low = lax.ppermute(
            lax.slice_in_dim(block, block.shape[dim] - width, None, axis=dim), axis, forward
        )
        high = lax.ppermute(lax.slice_in_dim(block, 0, width, axis=dim), axis, backward)
        block = jnp.concatenate([low, block, high], axis=dim)
    return block


def shifted(value, axis, steps):
    count = lax.axis_size(axis)
    first, last = (max(0, -steps), min(count, count - steps))
    return lax.ppermute(value, axis, [(source, source + steps) for source in range(first, last)])


def mult(left, right):
    return jnp.einsum("...ij,...jk->...ik", left, right, precision=lax.Precision.HIGHEST)


def inner(left, right):
    return jnp.einsum("...mz,...nz->...mn", left, right, precision=lax.Precision.HIGHEST)


def solve_lower(lower, values):
    return lax.linalg.triangular_solve(lower, values, left_side=True, lower=True)


def build_transfer(ritz, correlation):
    count = ritz.shape[-1]
    unit = jnp.eye(count, dtype=ritz.dtype)
    phase = phase_step * ritz
    square = mult(phase, phase)
    cosine = unit - 0.5 * square + mult(square, square) / 24.0
    sine = phase - mult(phase, square) / 6.0
    turned = mult(correlation, cosine)
    skewed = mult(correlation, sine)
    upper = jnp.concatenate([turned, -skewed], axis=-1)
    below = jnp.concatenate([skewed, turned], axis=-1)
    return jnp.concatenate([upper, below], axis=-2)


def local(freq_scale, base_profile, perturb, start_block, source):
    freqs = freq_scale.shape[0]
    seg_count = perturb.shape[0]
    modes = start_block.shape[0]
    alt_local = start_block.shape[1]
    alt_total = alt_local * lax.axis_size("alt")
    coef = (
        freq_scale[:, None, None, None]
        * (base_profile[None, :] * (1.0 + relief * perturb))[None, :, None, :]
    )

    def apply_operator(block):
        padded = with_halo(block, (("alt", 3),), 1)
        return coef * block + 0.5 * (padded[..., 2:] + padded[..., :-2])

    iter_count = ITERS
    basis = jnp.broadcast_to(
        start_block / jnp.sqrt(float(alt_total)), (freqs, seg_count) + start_block.shape
    )
    for step in range(iter_count):
        image = apply_operator(basis)
        gram = lax.psum(inner(image, image), "alt")
        basis = solve_lower(jnp.linalg.cholesky(gram), image)
    himage = apply_operator(basis)
    upcoming = shifted(basis[:, 0], "range", -1)
    ahead = jnp.concatenate([basis[:, 1:], upcoming[:, None]], axis=1)
    ritz, correlation = lax.psum((inner(basis, himage), inner(ahead, basis)), "alt")
    transfer = build_transfer(ritz, correlation)
    width = 2 * modes
    product = jnp.broadcast_to(jnp.eye(width, dtype=jnp.float32), (freqs, width, width))
    for seg in range(seg_count):
        product = mult(transfer[:, seg], product)
    start = jnp.concatenate([source[:, 0], source[:, 1]], axis=-1)
    position = lax.axis_index("range")
    carry = jnp.where(position == 0, start, jnp.zeros_like(start))

    def relay_step(turn, state):
        leaving = jnp.einsum("fij,fj->fi", product, state, precision=lax.Precision.HIGHEST)
        arrived = shifted(leaving, "range", 1)
        return jnp.where(position == turn + 1, arrived, state)

    carry = lax.fori_loop(0, lax.axis_size("range") - 1, relay_step, carry)
    amp_list = []
    state = carry
    for seg in range(seg_count):
        amp_list.append(state)
        if seg + 1 < seg_count:
            state = jnp.einsum(
                "fij,fj->fi", transfer[:, seg], state, precision=lax.Precision.HIGHEST
            )
    amps = jnp.stack(amp_list, axis=1).reshape(freqs, seg_count, 2, modes)
    scale = jnp.sqrt(float(alt_total) / float(modes))
    return scale * jnp.einsum("fspm,fsmz->fspz", amps, basis, precision=lax.Precision.HIGHEST)


def solution(mesh):
    in_specs = (P("freq"), P("alt"), P("range", "alt"), P(None, "alt"), P("freq", None, None))
    out_specs = P("freq", "range", None, "alt")
    return jax.shard_map(local, mesh=mesh, in_specs=in_specs, out_specs=out_specs, check_vma=False)
```

profile of v0, /device:TPU:8, one launch (start us, length us, event | category | flops | bytes accessed | tf_op | source)
XLA Modules:
  0.0 1563.9 jit_solution(673033635187756319)
XLA Ops:
  9.1 3.1 collective-permute-start.2
  13.7 2.5 fusion.77
  16.3 39.1 %all-reduce.11.cloned.1.call-done = f32[2,4,96,96]{2,3,1,0:T(8,128)} async-done(((f32[2,4,96,96]{2,3,1,0:T(8,128)}), f32[2,4,96,96]{2,3,1,0:T(8,128)}) %all-reduce.11.cloned.1.call-update) | async-done | bytes 294928 | tf_op jit(solution)/shard_map/psum | solution.py:77
  57.6 70.3 %custom-call.20 = f32[2,4,96,96]{3,2,1,0:T(8,128)S(1)} custom-call(f32[2,4,96,96]{3,2,1,0:T(8,128)S(1)} %fusion.64), custom_call_target="Cholesky" | custom-call | tf_op jit(solution)/shard_map/jit(cholesky)/cholesky | solution.py:78
  128.3 59.0 %custom-call.21 = f32[2,4,1,96,96]{3,4,2,1,0:T(8,128)S(1)} custom-call(f32[2,4,1,96,96]{4,3,2,1,0:T(8,128)S(1)} %select_bitcast_fusion.7), custom_call_target="InvertDiagBlocksLowerTriangular" | custom-call | tf_op jit(solution)/shard_map/triangular_solve/custom-call.0 | solution.py:39
  190.2 3.1 collective-permute-start.4
  194.5 2.5 fusion.105
  197.4 37.7 %all-reduce.13.cloned.1.call-done = f32[2,4,96,96]{2,3,1,0:T(8,128)} async-done(((f32[2,4,96,96]{2,3,1,0:T(8,128)}), f32[2,4,96,96]{2,3,1,0:T(8,128)}) %all-reduce.13.cloned.1.call-update) | async-done | bytes 294928 | tf_op jit(solution)/shard_map/psum | solution.py:77
  237.3 70.3 %custom-call.22 = f32[2,4,96,96]{3,2,1,0:T(8,128)S(1)} custom-call(f32[2,4,96,96]{3,2,1,0:T(8,128)S(1)} %fusion.61), custom_call_target="Cholesky" | custom-call | tf_op jit(solution)/shard_map/jit(cholesky)/cholesky | solution.py:78
  308.0 59.0 %custom-call.23 = f32[2,4,1,96,96]{3,4,2,1,0:T(8,128)S(1)} custom-call(f32[2,4,1,96,96]{4,3,2,1,0:T(8,128)S(1)} %select_bitcast_fusion.6), custom_call_target="InvertDiagBlocksLowerTriangular" | custom-call | tf_op jit(solution)/shard_map/triangular_solve/custom-call.0 | solution.py:39
  369.9 3.1 collective-permute-start.6
  374.3 2.5 fusion.108
  377.4 37.5 %all-reduce.15.cloned.1.call-done = f32[2,4,96,96]{2,3,1,0:T(8,128)} async-done(((f32[2,4,96,96]{2,3,1,0:T(8,128)}), f32[2,4,96,96]{2,3,1,0:T(8,128)}) %all-reduce.15.cloned.1.call-update) | async-done | bytes 294928 | tf_op jit(solution)/shard_map/psum | solution.py:77
  417.0 70.3 %custom-call.24 = f32[2,4,96,96]{3,2,1,0:T(8,128)S(1)} custom-call(f32[2,4,96,96]{3,2,1,0:T(8,128)S(1)} %fusion.58), custom_call_target="Cholesky" | custom-call | tf_op jit(solution)/shard_map/jit(cholesky)/cholesky | solution.py:78
  487.7 59.0 %custom-call.25 = f32[2,4,1,96,96]{3,4,2,1,0:T(8,128)S(1)} custom-call(f32[2,4,1,96,96]{4,3,2,1,0:T(8,128)S(1)} %select_bitcast_fusion.5), custom_call_target="InvertDiagBlocksLowerTriangular" | custom-call | tf_op jit(solution)/shard_map/triangular_solve/custom-call.0 | solution.py:39
  549.6 3.1 collective-permute-start.8
  554.0 2.5 fusion.111
  556.7 37.8 %all-reduce.17.cloned.1.call-done = f32[2,4,96,96]{2,3,1,0:T(8,128)} async-done(((f32[2,4,96,96]{2,3,1,0:T(8,128)}), f32[2,4,96,96]{2,3,1,0:T(8,128)}) %all-reduce.17.cloned.1.call-update) | async-done | bytes 294928 | tf_op jit(solution)/shard_map/psum | solution.py:77
  596.8 70.3 %custom-call.26 = f32[2,4,96,96]{3,2,1,0:T(8,128)S(1)} custom-call(f32[2,4,96,96]{3,2,1,0:T(8,128)S(1)} %fusion.55), custom_call_target="Cholesky" | custom-call | tf_op jit(solution)/shard_map/jit(cholesky)/cholesky | solution.py:78
  667.5 59.0 %custom-call.27 = f32[2,4,1,96,96]{3,4,2,1,0:T(8,128)S(1)} custom-call(f32[2,4,1,96,96]{4,3,2,1,0:T(8,128)S(1)} %select_bitcast_fusion.4), custom_call_target="InvertDiagBlocksLowerTriangular" | custom-call | tf_op jit(solution)/shard_map/triangular_solve/custom-call.0 | solution.py:39
  730.7 3.0 collective-permute-done.9
  733.7 2.5 fusion.114
  736.5 38.1 %all-reduce.19.cloned.1.call-done = f32[2,4,96,96]{2,3,1,0:T(8,128)} async-done(((f32[2,4,96,96]{2,3,1,0:T(8,128)}), f32[2,4,96,96]{2,3,1,0:T(8,128)}) %all-reduce.19.cloned.1.call-update) | async-done | bytes 294928 | tf_op jit(solution)/shard_map/psum | solution.py:77
  776.8 70.3 %custom-call.28 = f32[2,4,96,96]{3,2,1,0:T(8,128)S(1)} custom-call(f32[2,4,96,96]{3,2,1,0:T(8,128)S(1)} %fusion.52), custom_call_target="Cholesky" | custom-call | tf_op jit(solution)/shard_map/jit(cholesky)/cholesky | solution.py:78
  847.5 59.0 %custom-call.29 = f32[2,4,1,96,96]{3,4,2,1,0:T(8,128)S(1)} custom-call(f32[2,4,1,96,96]{4,3,2,1,0:T(8,128)S(1)} %select_bitcast_fusion.3), custom_call_target="InvertDiagBlocksLowerTriangular" | custom-call | tf_op jit(solution)/shard_map/triangular_solve/custom-call.0 | solution.py:39
  906.5 1.4 fusion.50
  909.4 3.1 collective-permute-start.12
  913.8 2.5 fusion.117
  916.6 37.8 %all-reduce.21.cloned.1.call-done = f32[2,4,96,96]{2,3,1,0:T(8,128)} async-done(((f32[2,4,96,96]{2,3,1,0:T(8,128)}), f32[2,4,96,96]{2,3,1,0:T(8,128)}) %all-reduce.21.cloned.1.call-update) | async-done | bytes 294928 | tf_op jit(solution)/shard_map/psum | solution.py:77
  956.5 70.3 %custom-call.30 = f32[2,4,96,96]{3,2,1,0:T(8,128)S(1)} custom-call(f32[2,4,96,96]{3,2,1,0:T(8,128)S(1)} %fusion.49), custom_call_target="Cholesky" | custom-call | tf_op jit(solution)/shard_map/jit(cholesky)/cholesky | solution.py:78
  1027.2 59.0 %custom-call.31 = f32[2,4,1,96,96]{3,4,2,1,0:T(8,128)S(1)} custom-call(f32[2,4,1,96,96]{4,3,2,1,0:T(8,128)S(1)} %select_bitcast_fusion.2), custom_call_target="InvertDiagBlocksLowerTriangular" | custom-call | tf_op jit(solution)/shard_map/triangular_solve/custom-call.0 | solution.py:39
  1089.1 3.1 collective-permute-start.14
  1093.5 2.5 fusion.120
  1096.4 37.7 %all-reduce.23.cloned.1.call-done = f32[2,4,96,96]{2,3,1,0:T(8,128)} async-done(((f32[2,4,96,96]{2,3,1,0:T(8,128)}), f32[2,4,96,96]{2,3,1,0:T(8,128)}) %all-reduce.23.cloned.1.call-update) | async-done | bytes 294928 | tf_op jit(solution)/shard_map/psum | solution.py:77
  1136.3 70.3 %custom-call.32 = f32[2,4,96,96]{3,2,1,0:T(8,128)S(1)} custom-call(f32[2,4,96,96]{3,2,1,0:T(8,128)S(1)} %fusion.46), custom_call_target="Cholesky" | custom-call | tf_op jit(solution)/shard_map/jit(cholesky)/cholesky | solution.py:78
  1206.9 59.0 %custom-call.33 = f32[2,4,1,96,96]{3,4,2,1,0:T(8,128)S(1)} custom-call(f32[2,4,1,96,96]{4,3,2,1,0:T(8,128)S(1)} %select_bitcast_fusion.1), custom_call_target="InvertDiagBlocksLowerTriangular" | custom-call | tf_op jit(solution)/shard_map/triangular_solve/custom-call.0 | solution.py:39
  1268.9 3.1 collective-permute-start.16
  1273.2 2.5 fusion.123
  1276.3 37.5 %all-reduce.25.cloned.1.call-done = f32[2,4,96,96]{2,3,1,0:T(8,128)} async-done(((f32[2,4,96,96]{2,3,1,0:T(8,128)}), f32[2,4,96,96]{2,3,1,0:T(8,128)}) %all-reduce.25.cloned.1.call-update) | async-done | bytes 294928 | tf_op jit(solution)/shard_map/psum | solution.py:77
  1316.0 70.3 %custom-call.34 = f32[2,4,96,96]{3,2,1,0:T(8,128)S(1)} custom-call(f32[2,4,96,96]{3,2,1,0:T(8,128)S(1)} %fusion.43), custom_call_target="Cholesky" | custom-call | tf_op jit(solution)/shard_map/jit(cholesky)/cholesky | solution.py:78
  1386.7 59.0 %custom-call.35 = f32[2,4,1,96,96]{3,4,2,1,0:T(8,128)S(1)} custom-call(f32[2,4,1,96,96]{4,3,2,1,0:T(8,128)S(1)} %select_bitcast_fusion), custom_call_target="InvertDiagBlocksLowerTriangular" | custom-call | tf_op jit(solution)/shard_map/triangular_solve/custom-call.0 | solution.py:39
  1448.6 3.1 collective-permute-start.19
  1451.7 3.5 collective-permute-start.17
  1455.3 2.0 fusion.7
  1457.3 3.2 collective-permute-done.17
  1460.5 1.6 fusion.35
  1462.3 34.7 %all-reduce.27.cloned.1.call-done = (f32[2,4,96,96]{3,2,1,0:T(8,128)}, f32[2,4,96,96]{3,2,1,0:T(8,128)}) async-done(((f32[2,4,96,96]{3,2,1,0:T(8,128)}, f32[2,4,96,96]{3,2,1,0:T(8,128)}), (f32[2,4,96,96]{3,2,1,0:T(8,128)}, f32[2,4,96,96]{3,2,1,0:T(8,128)})) %all-reduce.27.cloned.1.call-update) | async-done | bytes 589840 | tf_op jit(solution)/shard_map/psum | solution.py:82
  1497.0 1.7 fusion.74
  1498.8 1.7 fusion.2
  1506.9 47.9 %while.13 = (s32[]{:T(128)}, f32[2,192]{1,0:T(2,128)S(1)}, s32[]{:T(128)}, f32[2,192,192]{2,1,0:T(8,128)S(1)}, s32[]{:T(128)}) while((s32[]{:T(128)}, f32[2,192]{1,0:T(2,128)S(1)}, s32[]{:T(128)}, f32[2,192,192]{2,1,0:T(8,128)S(1)}, s32[]{:T(128)}) %tuple.45), condition=%wide.region_13.16_spmd, body=%wide.region_12.15_spmd.sunk | while | flops 885123 | bytes 311919 | solution.py:97
  1507.4 3.4 collective-permute-start
  1510.8 3.0 collective-permute-done
  1514.2 2.5 collective-permute-start
  1516.7 3.9 collective-permute-done
  1521.0 1.9 collective-permute-start
  1523.0 4.4 collective-permute-done
  1527.9 1.9 collective-permute-start
  1529.8 4.4 collective-permute-done
  1534.7 1.9 collective-permute-start
  1536.6 4.4 collective-permute-done
  1541.5 1.9 collective-permute-start
  1543.5 4.4 collective-permute-done
  1548.4 1.9 collective-permute-start
  1550.3 4.4 collective-permute-done
  (159 shorter events, 69.9 us)
Async XLA Ops:
  6.5 48.8 %all-reduce.11.cloned.1.call-start = ((), (), s32[]{:S(2)}) async-start(), calls=%async_computation | async-start | bytes 786432 | tf_op jit(solution)/shard_map/psum | solution.py:77
  7.7 5.9 collective-permute-start.1
  9.1 4.5 collective-permute-start.2
  16.2 218.9 %all-reduce.13.cloned.1.call-start = ((), (), s32[]{:S(2)}) async-start(), calls=%async_computation.1 | async-start | bytes 786432 | tf_op jit(solution)/shard_map/psum | solution.py:77
  188.9 4.4 collective-permute-start.3
  190.2 4.4 collective-permute-start.4
  197.0 217.8 %all-reduce.15.cloned.1.call-start = ((), (), s32[]{:S(2)}) async-start(), calls=%async_computation.2 | async-start | bytes 786432 | tf_op jit(solution)/shard_map/psum | solution.py:77
  368.6 4.4 collective-permute-start.5
  369.9 4.4 collective-permute-start.6
  376.8 217.8 %all-reduce.17.cloned.1.call-start = ((), (), s32[]{:S(2)}) async-start(), calls=%async_computation.3 | async-start | bytes 786432 | tf_op jit(solution)/shard_map/psum | solution.py:77
  548.3 4.4 collective-permute-start.7
  549.6 4.4 collective-permute-start.8
  556.5 218.1 %all-reduce.19.cloned.1.call-start = ((), (), s32[]{:S(2)}) async-start(), calls=%async_computation.4 | async-start | bytes 786432 | tf_op jit(solution)/shard_map/psum | solution.py:77
  728.1 2.6 collective-permute-start.10
  729.4 4.3 collective-permute-start.9
  736.2 218.1 %all-reduce.21.cloned.1.call-start = ((), (), s32[]{:S(2)}) async-start(), calls=%async_computation.5 | async-start | bytes 786432 | tf_op jit(solution)/shard_map/psum | solution.py:77
  908.1 4.4 collective-permute-start.11
  909.4 4.4 collective-permute-start.12
  916.3 217.8 %all-reduce.23.cloned.1.call-start = ((), (), s32[]{:S(2)}) async-start(), calls=%async_computation.6 | async-start | bytes 786432 | tf_op jit(solution)/shard_map/psum | solution.py:77
  1087.8 4.4 collective-permute-start.13
  1089.1 4.4 collective-permute-start.14
  1096.0 217.8 %all-reduce.25.cloned.1.call-start = ((), (), s32[]{:S(2)}) async-start(), calls=%async_computation.7 | async-start | bytes 786432 | tf_op jit(solution)/shard_map/psum | solution.py:77
  1267.6 8.8 copy-start.1
  1267.6 4.4 collective-permute-start.15
  1268.9 4.4 collective-permute-start.16
  1275.7 221.3 %all-reduce.27.cloned.1.call-start = ((), (), s32[]{:S(2)}) async-start(), calls=%async_computation.8 | async-start | bytes 1572864 | tf_op jit(solution)/shard_map/psum | solution.py:82
  1447.3 8.0 collective-permute-start.18
  1448.6 6.7 collective-permute-start.19
  1451.7 8.8 collective-permute-start.17
  1497.0 3.9 copy-start
  1507.4 6.4 collective-permute-start
  1514.2 6.4 collective-permute-start
  1521.0 6.4 collective-permute-start
  1527.9 6.4 collective-permute-start
  1534.7 6.4 collective-permute-start
  1541.5 6.4 collective-permute-start
  1548.4 6.4 collective-permute-start
Sparse Core Ops, SparseCore 0:
  16.3 38.9 all-reduce.10
  197.2 37.8 all-reduce.12
  376.9 37.8 all-reduce.14
  556.6 37.8 all-reduce.16
  736.3 38.2 all-reduce.18
  916.4 37.8 all-reduce.20
  1096.1 37.8 all-reduce.22
  1275.9 37.8 all-reduce.24
  1462.3 34.6 all-reduce.26
where the time goes:
time: 1570 us; the launch traced here: 1560 us
  other arithmetic  1050 us (67%)
  waiting for transfers between devices  381 us (24%)
  starting transfers between devices  59 us (4%)
  matrix products  49.2 us (3%)
    another operation x25, other arithmetic, local(): basis = solve_lower(jnp.linalg.cholesky(gram), image)  564 us
    another operation x17, other arithmetic, solve_lower(): lax.linalg.triangular_solve(lower, values, left_side=True, lower=True)  473 us
    psum x8, waiting for transfers between devices, local(): gram = lax.psum(inner(image, image), 'alt')  303 us
    psum x1, waiting for transfers between devices, local(): lax.psum((inner(basis, himage), inner(ahead, basis)), 'alt')  34.7 us
    ppermute x8, waiting for transfers between devices, shifted(): lax.ppermute(value, axis, [(source, source + steps) for source in range(f...  32.3 us
  transfers between devices with their start and end apart: 35, of which 24 were waited for; matrix products, arithmetic and copies ran while one was open for 0% of the time, Pallas kernels for 0%

commit v1 on v0

--- a/solution.py
+++ b/solution.py
@@ -74,7 +74,7 @@
     )
     for step in range(iter_count):
         image = apply_operator(basis)
-        gram = lax.psum(inner(image, image), "alt")
+        gram = jnp.sum(lax.all_gather(inner(image, image), "alt"), axis=0)
         basis = solve_lower(jnp.linalg.cholesky(gram), image)
     himage = apply_operator(basis)
     upcoming = shifted(basis[:, 0], "range", -1)

time: 1570 us -> 1470 us (0.936)
  waiting for transfers between devices: 381 us -> 286 us
    psum x8 -> x0, waiting for transfers between devices: 303 us -> none  [local(): gram = lax.psum(inner(image, image), 'alt')]
    all_gather x0 -> x8, waiting for transfers between devices: none -> 208 us  [local(): gram = jnp.sum(lax.all_gather(inner(image, image), 'alt'), axis=0)]
where the time goes in v1:
time: 1470 us
  other arithmetic  1050 us (71%)
  waiting for transfers between devices  286 us (19%)
  starting transfers between devices  59.8 us (4%)
  matrix products  49.4 us (3%)
    another operation x25, other arithmetic, local(): basis = solve_lower(jnp.linalg.cholesky(gram), image)  564 us
    another operation x17, other arithmetic, solve_lower(): lax.linalg.triangular_solve(lower, values, left_side=True, lower=True)  473 us
    all_gather x8, waiting for transfers between devices, local(): gram = jnp.sum(lax.all_gather(inner(image, image), 'alt'), axis=0)  208 us
    psum x1, waiting for transfers between devices, local(): lax.psum((inner(basis, himage), inner(ahead, basis)), 'alt')  35.4 us
    ppermute x8, waiting for transfers between devices, shifted(): lax.ppermute(value, axis, [(source, source + steps) for source in range(f...  32.6 us
  transfers between devices with their start and end apart: 35, of which 24 were waited for; matrix products, arithmetic and copies ran while one was open for 0% of the time, Pallas kernels for 0%

profile of v1, /device:TPU:8, one launch (start us, length us, event | category | flops | bytes accessed | tf_op | source)
XLA Modules:
  0.0 1466.7 jit_solution(5362007830544784050)
XLA Ops:
  9.1 3.1 collective-permute-start.2
  13.7 2.5 fusion.77
  16.3 26.1 %all-gather.17.cloned.1.call-done = f32[8,4,96,96]{3,2,1,0:T(8,128)} async-done(((f32[2,4,96,96]{3,2,1,0:T(8,128)}), f32[8,4,96,96]{3,2,1,0:T(8,128)}) %all-gather.17.cloned.1.call-update) | async-done | bytes 1179664 | tf_op jit(solution)/shard_map/all_gather | solution.py:77
  44.2 70.3 %custom-call.20 = f32[2,4,96,96]{3,2,1,0:T(8,128)S(1)} custom-call(f32[2,4,96,96]{3,2,1,0:T(8,128)S(1)} %fusion.64), custom_call_target="Cholesky" | custom-call | tf_op jit(solution)/shard_map/jit(cholesky)/cholesky | solution.py:78
  114.9 59.0 %custom-call.21 = f32[2,4,1,96,96]{3,4,2,1,0:T(8,128)S(1)} custom-call(f32[2,4,1,96,96]{4,3,2,1,0:T(8,128)S(1)} %select_bitcast_fusion.7), custom_call_target="InvertDiagBlocksLowerTriangular" | custom-call | tf_op jit(solution)/shard_map/triangular_solve/custom-call.0 | solution.py:39
  176.8 3.1 collective-permute-start.4
  181.2 2.5 fusion.105
  184.1 26.1 %all-gather.19.cloned.1.call-done = f32[8,4,96,96]{3,2,1,0:T(8,128)} async-done(((f32[2,4,96,96]{3,2,1,0:T(8,128)}), f32[8,4,96,96]{3,2,1,0:T(8,128)}) %all-gather.19.cloned.1.call-update) | async-done | bytes 1179664 | tf_op jit(solution)/shard_map/all_gather | solution.py:77
  212.0 70.3 %custom-call.22 = f32[2,4,96,96]{3,2,1,0:T(8,128)S(1)} custom-call(f32[2,4,96,96]{3,2,1,0:T(8,128)S(1)} %fusion.61), custom_call_target="Cholesky" | custom-call | tf_op jit(solution)/shard_map/jit(cholesky)/cholesky | solution.py:78
  282.7 59.0 %custom-call.23 = f32[2,4,1,96,96]{3,4,2,1,0:T(8,128)S(1)} custom-call(f32[2,4,1,96,96]{4,3,2,1,0:T(8,128)S(1)} %select_bitcast_fusion.6), custom_call_target="InvertDiagBlocksLowerTriangular" | custom-call | tf_op jit(solution)/shard_map/triangular_solve/custom-call.0 | solution.py:39
  344.6 3.1 collective-permute-start.6
  349.0 2.5 fusion.108
  352.1 25.9 %all-gather.21.cloned.1.call-done = f32[8,4,96,96]{3,2,1,0:T(8,128)} async-done(((f32[2,4,96,96]{3,2,1,0:T(8,128)}), f32[8,4,96,96]{3,2,1,0:T(8,128)}) %all-gather.21.cloned.1.call-update) | async-done | bytes 1179664 | tf_op jit(solution)/shard_map/all_gather | solution.py:77
  379.8 70.3 %custom-call.24 = f32[2,4,96,96]{3,2,1,0:T(8,128)S(1)} custom-call(f32[2,4,96,96]{3,2,1,0:T(8,128)S(1)} %fusion.58), custom_call_target="Cholesky" | custom-call | tf_op jit(solution)/shard_map/jit(cholesky)/cholesky | solution.py:78
  450.5 59.0 %custom-call.25 = f32[2,4,1,96,96]{3,4,2,1,0:T(8,128)S(1)} custom-call(f32[2,4,1,96,96]{4,3,2,1,0:T(8,128)S(1)} %select_bitcast_fusion.5), custom_call_target="InvertDiagBlocksLowerTriangular" | custom-call | tf_op jit(solution)/shard_map/triangular_solve/custom-call.0 | solution.py:39
  512.4 3.1 collective-permute-start.8
  516.7 2.5 fusion.111
  519.5 26.2 %all-gather.23.cloned.1.call-done = f32[8,4,96,96]{3,2,1,0:T(8,128)} async-done(((f32[2,4,96,96]{3,2,1,0:T(8,128)}), f32[8,4,96,96]{3,2,1,0:T(8,128)}) %all-gather.23.cloned.1.call-update) | async-done | bytes 1179664 | tf_op jit(solution)/shard_map/all_gather | solution.py:77
  547.5 70.3 %custom-call.26 = f32[2,4,96,96]{3,2,1,0:T(8,128)S(1)} custom-call(f32[2,4,96,96]{3,2,1,0:T(8,128)S(1)} %fusion.55), custom_call_target="Cholesky" | custom-call | tf_op jit(solution)/shard_map/jit(cholesky)/cholesky | solution.py:78
  618.2 59.0 %custom-call.27 = f32[2,4,1,96,96]{3,4,2,1,0:T(8,128)S(1)} custom-call(f32[2,4,1,96,96]{4,3,2,1,0:T(8,128)S(1)} %select_bitcast_fusion.4), custom_call_target="InvertDiagBlocksLowerTriangular" | custom-call | tf_op jit(solution)/shard_map/triangular_solve/custom-call.0 | solution.py:39
  678.8 2.2 collective-permute-start.10
  682.3 2.3 collective-permute-done.9
  684.6 2.5 fusion.114
  687.4 25.1 %all-gather.25.cloned.1.call-done = f32[8,4,96,96]{3,2,1,0:T(8,128)} async-done(((f32[2,4,96,96]{3,2,1,0:T(8,128)}), f32[8,4,96,96]{3,2,1,0:T(8,128)}) %all-gather.25.cloned.1.call-update) | async-done | bytes 1179664 | tf_op jit(solution)/shard_map/all_gather | solution.py:77
  714.3 70.3 %custom-call.28 = f32[2,4,96,96]{3,2,1,0:T(8,128)S(1)} custom-call(f32[2,4,96,96]{3,2,1,0:T(8,128)S(1)} %fusion.52), custom_call_target="Cholesky" | custom-call | tf_op jit(solution)/shard_map/jit(cholesky)/cholesky | solution.py:78
  785.0 59.0 %custom-call.29 = f32[2,4,1,96,96]{3,4,2,1,0:T(8,128)S(1)} custom-call(f32[2,4,1,96,96]{4,3,2,1,0:T(8,128)S(1)} %select_bitcast_fusion.3), custom_call_target="InvertDiagBlocksLowerTriangular" | custom-call | tf_op jit(solution)/shard_map/triangular_solve/custom-call.0 | solution.py:39
  846.9 3.1 collective-permute-start.12
  851.3 2.5 fusion.117
  854.1 26.2 %all-gather.27.cloned.1.call-done = f32[8,4,96,96]{3,2,1,0:T(8,128)} async-done(((f32[2,4,96,96]{3,2,1,0:T(8,128)}), f32[8,4,96,96]{3,2,1,0:T(8,128)}) %all-gather.27.cloned.1.call-update) | async-done | bytes 1179664 | tf_op jit(solution)/shard_map/all_gather | solution.py:77
  882.1 70.3 %custom-call.30 = f32[2,4,96,96]{3,2,1,0:T(8,128)S(1)} custom-call(f32[2,4,96,96]{3,2,1,0:T(8,128)S(1)} %fusion.49), custom_call_target="Cholesky" | custom-call | tf_op jit(solution)/shard_map/jit(cholesky)/cholesky | solution.py:78
  952.8 59.0 %custom-call.31 = f32[2,4,1,96,96]{3,4,2,1,0:T(8,128)S(1)} custom-call(f32[2,4,1,96,96]{4,3,2,1,0:T(8,128)S(1)} %select_bitcast_fusion.2), custom_call_target="InvertDiagBlocksLowerTriangular" | custom-call | tf_op jit(solution)/shard_map/triangular_solve/custom-call.0 | solution.py:39
  1014.7 3.1 collective-permute-start.14
  1019.1 2.5 fusion.120
  1022.1 25.9 %all-gather.29.cloned.1.call-done = f32[8,4,96,96]{3,2,1,0:T(8,128)} async-done(((f32[2,4,96,96]{3,2,1,0:T(8,128)}), f32[8,4,96,96]{3,2,1,0:T(8,128)}) %all-gather.29.cloned.1.call-update) | async-done | bytes 1179664 | tf_op jit(solution)/shard_map/all_gather | solution.py:77
  1049.9 70.3 %custom-call.32 = f32[2,4,96,96]{3,2,1,0:T(8,128)S(1)} custom-call(f32[2,4,96,96]{3,2,1,0:T(8,128)S(1)} %fusion.46), custom_call_target="Cholesky" | custom-call | tf_op jit(solution)/shard_map/jit(cholesky)/cholesky | solution.py:78
  1120.5 59.0 %custom-call.33 = f32[2,4,1,96,96]{3,4,2,1,0:T(8,128)S(1)} custom-call(f32[2,4,1,96,96]{4,3,2,1,0:T(8,128)S(1)} %select_bitcast_fusion.1), custom_call_target="InvertDiagBlocksLowerTriangular" | custom-call | tf_op jit(solution)/shard_map/triangular_solve/custom-call.0 | solution.py:39
  1182.5 3.1 collective-permute-start.16
  1186.8 2.5 fusion.123
  1189.6 26.2 %all-gather.31.cloned.1.call-done = f32[8,4,96,96]{3,2,1,0:T(8,128)} async-done(((f32[2,4,96,96]{3,2,1,0:T(8,128)}), f32[8,4,96,96]{3,2,1,0:T(8,128)}) %all-gather.31.cloned.1.call-update) | async-done | bytes 1179664 | tf_op jit(solution)/shard_map/all_gather | solution.py:77
  1217.6 70.3 %custom-call.34 = f32[2,4,96,96]{3,2,1,0:T(8,128)S(1)} custom-call(f32[2,4,96,96]{3,2,1,0:T(8,128)S(1)} %fusion.43), custom_call_target="Cholesky" | custom-call | tf_op jit(solution)/shard_map/jit(cholesky)/cholesky | solution.py:78
  1288.3 59.0 %custom-call.35 = f32[2,4,1,96,96]{3,4,2,1,0:T(8,128)S(1)} custom-call(f32[2,4,1,96,96]{4,3,2,1,0:T(8,128)S(1)} %select_bitcast_fusion), custom_call_target="InvertDiagBlocksLowerTriangular" | custom-call | tf_op jit(solution)/shard_map/triangular_solve/custom-call.0 | solution.py:39
  1350.2 3.1 collective-permute-start.19
  1353.4 3.6 collective-permute-start.17
  1357.0 2.0 fusion.7
  1359.0 3.6 collective-permute-done.17
  1362.6 1.6 fusion.35
  1364.4 35.4 %all-reduce.3.cloned.1.call-done = (f32[2,4,96,96]{3,2,1,0:T(8,128)}, f32[2,4,96,96]{3,2,1,0:T(8,128)}) async-done(((f32[2,4,96,96]{3,2,1,0:T(8,128)}, f32[2,4,96,96]{3,2,1,0:T(8,128)}), (f32[2,4,96,96]{3,2,1,0:T(8,128)}, f32[2,4,96,96]{3,2,1,0:T(8,128)})) %all-reduce.3.cloned.1.call-update) | async-done | bytes 589840 | tf_op jit(solution)/shard_map/psum | solution.py:82
  1399.8 1.7 fusion.74
  1401.5 1.7 fusion.2
  1409.7 47.9 %while.13 = (s32[]{:T(128)}, f32[2,192]{1,0:T(2,128)S(1)}, s32[]{:T(128)}, f32[2,192,192]{2,1,0:T(8,128)S(1)}, s32[]{:T(128)}) while((s32[]{:T(128)}, f32[2,192]{1,0:T(2,128)S(1)}, s32[]{:T(128)}, f32[2,192,192]{2,1,0:T(8,128)S(1)}, s32[]{:T(128)}) %tuple.45), condition=%wide.region_13.16_spmd, body=%wide.region_12.15_spmd.sunk | while | flops 885123 | bytes 311919 | solution.py:97
  1410.1 3.4 collective-permute-start
  1413.6 3.0 collective-permute-done
  1417.0 2.5 collective-permute-start
  1419.5 3.9 collective-permute-done
  1423.8 1.9 collective-permute-start
  1425.7 4.4 collective-permute-done
  1430.6 1.9 collective-permute-start
  1432.6 4.4 collective-permute-done
  1437.5 1.9 collective-permute-start
  1439.4 4.4 collective-permute-done
  1444.3 1.9 collective-permute-start
  1446.2 4.4 collective-permute-done
  1451.1 1.9 collective-permute-start
  1453.1 4.4 collective-permute-done
  (167 shorter events, 66.6 us)
Async XLA Ops:
  6.5 35.9 %all-gather.17.cloned.1.call-start = ((), (), s32[]{:S(2)}) async-start(), calls=%async_computation | async-start | bytes 1966080 | tf_op jit(solution)/shard_map/all_gather | solution.py:77
  7.7 5.9 collective-permute-start.1
  9.1 4.5 collective-permute-start.2
  16.2 194.0 %all-gather.19.cloned.1.call-start = ((), (), s32[]{:S(2)}) async-start(), calls=%async_computation.1 | async-start | bytes 1966080 | tf_op jit(solution)/shard_map/all_gather | solution.py:77
  175.5 4.4 collective-permute-start.3
  176.8 4.4 collective-permute-start.4
  183.7 194.2 %all-gather.21.cloned.1.call-start = ((), (), s32[]{:S(2)}) async-start(), calls=%async_computation.2 | async-start | bytes 1966080 | tf_op jit(solution)/shard_map/all_gather | solution.py:77
  343.3 4.4 collective-permute-start.5
  344.6 4.4 collective-permute-start.6
  351.5 194.2 %all-gather.23.cloned.1.call-start = ((), (), s32[]{:S(2)}) async-start(), calls=%async_computation.3 | async-start | bytes 1966080 | tf_op jit(solution)/shard_map/all_gather | solution.py:77
  511.1 4.4 collective-permute-start.7
  512.4 4.4 collective-permute-start.8
  519.3 193.2 %all-gather.25.cloned.1.call-start = ((), (), s32[]{:S(2)}) async-start(), calls=%async_computation.4 | async-start | bytes 1966080 | tf_op jit(solution)/shard_map/all_gather | solution.py:77
  678.8 3.5 collective-permute-start.10
  681.0 3.6 collective-permute-start.9
  687.1 193.1 %all-gather.27.cloned.1.call-start = ((), (), s32[]{:S(2)}) async-start(), calls=%async_computation.5 | async-start | bytes 1966080 | tf_op jit(solution)/shard_map/all_gather | solution.py:77
  845.6 4.4 collective-permute-start.11
  846.9 4.4 collective-permute-start.12
  853.8 194.2 %all-gather.29.cloned.1.call-start = ((), (), s32[]{:S(2)}) async-start(), calls=%async_computation.6 | async-start | bytes 1966080 | tf_op jit(solution)/shard_map/all_gather | solution.py:77
  1013.4 4.4 collective-permute-start.13
  1014.7 4.4 collective-permute-start.14
  1021.6 194.2 %all-gather.31.cloned.1.call-start = ((), (), s32[]{:S(2)}) async-start(), calls=%async_computation.7 | async-start | bytes 1966080 | tf_op jit(solution)/shard_map/all_gather | solution.py:77
  1181.2 8.4 copy-start.1
  1181.2 4.4 collective-permute-start.15
  1182.5 4.4 collective-permute-start.16
  1189.4 210.5 %all-reduce.3.cloned.1.call-start = ((), (), s32[]{:S(2)}) async-start(), calls=%async_computation.8 | async-start | bytes 1572864 | tf_op jit(solution)/shard_map/psum | solution.py:82
  1348.9 8.0 collective-permute-start.18
  1350.2 6.7 collective-permute-start.19
  1353.4 9.3 collective-permute-start.17
  1399.8 3.9 copy-start
  1410.1 6.4 collective-permute-start
  1417.0 6.4 collective-permute-start
  1423.8 6.4 collective-permute-start
  1430.6 6.4 collective-permute-start
  1437.5 6.4 collective-permute-start
  1444.3 6.4 collective-permute-start
  1451.1 6.4 collective-permute-start
Sparse Core Ops, SparseCore 0:
  16.3 26.0 all-gather.16
  183.8 26.2 all-gather.18
  351.6 26.2 all-gather.20
  519.4 26.2 all-gather.22
  687.3 25.1 all-gather.24
  853.9 26.2 all-gather.26
  1021.7 26.2 all-gather.28
  1189.5 26.2 all-gather.30
  1364.4 35.3 all-reduce.2
